TPU v7x, 32 devices: a whole 2x2x4 slice. The times are simulated.
32 devices in a mesh: gx: 16 (over z, x, core), gy: 2 (over y).
Axes of the slice: x: 2, y: 2, z: 4, core: 2. Of those that a mesh axis runs over, the one named last changes fastest.
Arguments:
- particles: float32 [64, 2, 64, 1024], P(None, None, 'gx', 'gy'), may hold values from -32 to 32, as said below
- background: float32 [2, 64, 1024], P(None, 'gx', 'gy'), may hold values from -6 to 6
- obs_tile: int32 [16, 256], P('gx', 'gy'), may hold values from 0 to 127
- obs_mask: int32 [16, 16, 256], P(None, 'gx', 'gy'), may hold values 0 or 1
- obs_value: float32 [16, 256], P('gx', 'gy'), may hold values from -6 to 6
- obs_var: float32 [16, 256], P('gx', 'gy'), may hold values from 0.1 to 1
Outputs:
- analysis: float32 [64, 2, 64, 1024], P(None, None, 'gx', 'gy')
Inputs may be any that keep to these rules, and one draw needn't show every extreme that they name: `particles`: each particle is a field of order one to a few. `obs_tile`: an observation's value names tile row t // 128 and tile column t % (128) of its slab.
All inputs are finite; a program needn't handle non-finite values. No bound on the sum of `obs_mask` on one device may be relied on, other than what follows from the above.
Results may differ from a plain program's by a relative error of at most 0.0001.
Values sent between devices are 32-bit elements; how exact they have to be, the bound alone decides.
A program may use at most 64 MiB of HBM per device.

v0:
```python
import jax
import jax.numpy as jnp
from jax import lax
from jax.sharding import PartitionSpec as P

STEPS = 2
TILE = 4
lap_weight = 0.25
prior_weight = 0.05
couple_weight = 0.5
step_length = 1.0
epsilon = 1e-06
highest = lax.Precision.HIGHEST


def with_halo(block, sides, width):
    for axis, dim in sides:
        count = lax.axis_size(axis)
        forward = [(i, i + 1) for i in range(count - 1)]
        forward.append((count - 1, 0))
        backward = [(target, source) for source, target in forward]
        low = lax.ppermute(
            lax.slice_in_dim(block, block.shape[dim] - width, None, axis=dim), axis, forward
        )
        high = lax.ppermute(lax.slice_in_dim(block, 0, width, axis=dim), axis, backward)
        block = jnp.concatenate([low, block, high], axis=dim)
    return block


def laplace_inner(field):
    total = field[..., 1:-1, 2:] + field[..., 1:-1, :-2]
    total = total + field[..., 2:, 1:-1] + field[..., :-2, 1:-1]
    return total - 4.0 * field[..., 1:-1, 1:-1]


def prior_term(deviation):
    padded = with_halo(deviation, (("gx", 2), ("gy", 3)), 2)
    smooth = padded[..., 1:-1, 1:-1] - lap_weight * laplace_inner(padded)
    curved = smooth[..., 1:-1, 1:-1] - lap_weight * laplace_inner(smooth)
    return -prior_weight * (curved + couple_weight * (deviation - deviation[:, ::-1]))


def observe_term(state, table, weights, values, variance):
    count, rows, cols = (state.shape[0], state.shape[2], state.shape[3])
    tile_rows, tile_cols = (rows // TILE, cols // TILE)
    upper = state[:, 0].reshape(count, tile_rows, TILE, tile_cols, TILE)
    cells = upper.transpose(2, 4, 0, 1, 3).reshape(TILE * TILE, count, tile_rows * tile_cols)
    picked = jnp.einsum("cpt,ot->cpo", cells, table, precision=highest)
    mapped = 0.25 * jnp.sum(weights[:, None, :] * picked, axis=0)
    innovation = (values[None, :] - mapped) / variance[None, :]
    contrib = (0.25 * weights)[:, None, :] * innovation[None]
    spread = jnp.einsum("cpo,ot->cpt", contrib, table, precision=highest)
    back = spread.reshape(TILE, TILE, count, tile_rows, tile_cols).transpose(2, 3, 0, 4, 1)
    back = back.reshape(count, rows, cols)
    return jnp.stack([back, jnp.zeros_like(back)], axis=1)


def norm_scale(drift, denominator):
    total = lax.psum(jnp.sum(drift * drift), ("gx", "gy"))
    return step_length / jnp.sqrt(total / denominator + epsilon)


def per_device(particles, background, obs_tile, obs_mask, obs_value, obs_var):
    count = particles.shape[0]
    tiles = particles.shape[2] // TILE * (particles.shape[3] // TILE)
    table = (obs_tile[0][:, None] == jnp.arange(tiles, dtype=jnp.int32)[None, :]).astype(
        jnp.float32
    )
    weights = obs_mask[:, 0, :].astype(jnp.float32)
    values = obs_value[0]
    variance = obs_var[0]
    local_size = particles[0].size
    total_size = float(local_size * lax.axis_size("gx") * lax.axis_size("gy"))
    pair_count = float(count * (count - 1))
    off_diag = 1.0 - jnp.eye(count, dtype=jnp.float32)
    state = particles
    gram = None
    for step in range(STEPS):
        deviation = state - background[None]
        flat_dev = deviation.reshape(count, -1)
        if gram is None:
            gram = lax.psum(jnp.dot(flat_dev, flat_dev.T, precision=highest), ("gx", "gy"))
        gradient = prior_term(deviation) + observe_term(state, table, weights, values, variance)
        flat_grad = gradient.reshape(count, -1)
        diagonal = jnp.diagonal(gram)
        distance = diagonal[:, None] + diagonal[None, :] - 2.0 * gram
        width = jnp.sum(distance * off_diag) / (pair_count * total_size) + epsilon
        kernel = jnp.exp(-distance / (2.0 * width * total_size))
        attract = jnp.dot(kernel, flat_grad, precision=highest)
        pulled = jnp.dot(kernel, flat_dev, precision=highest)
        drift = (attract + (jnp.sum(kernel, axis=1)[:, None] * flat_dev - pulled) / width) / count
        if step + 1 < STEPS:
            cross, square = lax.psum(
                (
                    jnp.dot(flat_dev, drift.T, precision=highest),
                    jnp.dot(drift, drift.T, precision=highest),
                ),
                ("gx", "gy"),
            )
            scale = step_length / jnp.sqrt(jnp.trace(square) / (count * total_size) + epsilon)
            gram = gram + scale * (cross + cross.T) + scale * scale * square
        else:
            scale = norm_scale(drift, count * total_size)
        state = state + scale * drift.reshape(state.shape)
    return state


def solution(mesh):
    return jax.shard_map(
        per_device,
        mesh=mesh,
        in_specs=(
            P(None, None, "gx", "gy"),
            P(None, "gx", "gy"),
            P("gx", "gy"),
            P(None, "gx", "gy"),
            P("gx", "gy"),
            P("gx", "gy"),
        ),
        out_specs=P(None, None, "gx", "gy"),
        check_vma=False,
    )
```

profile of v0, /device:TPU:14, one launch (start us, length us, event | category | flops | bytes accessed | tf_op | source)
XLA Modules:
  0.0 223.9 jit_solution(16743643375088304163)
XLA Ops:
  0.0 2.8 %copy.40 = f32[64,2,4,512]{0,3,2,1:T(8,128)} copy(f32[64,2,4,512]{3,2,1,0:T(4,128)} %param.6) | data formatting | bytes 2097152 | tf_op args[0]
  2.8 2.2 broadcast_subtract_fusion.1
  6.1 2.4 %copy.32 = f32[64,2,2,512]{3,0,2,1:T(8,128)} copy(f32[64,2,2,512]{0,3,2,1:T(8,128)} %get-tuple-element.15) | data formatting | bytes 1048576 | tf_op jit(solution)/shard_map/slice | solution.py:23
  13.2 3.6 %convolution_bitcast_fusion.1 = f32[64,64]{1,0:T(8,128)S(1)} fusion(f32[64,2,4,512]{0,3,2,1:T(8,128)S(1)} %broadcast_subtract_fusion.1), kind=kOutput, calls=%fused_computation.61 | convolution fusion | flops 201326592 | bytes 1064960 | tf_op jit(solution)/shard_map/dot_general | solution.py:82
  19.3 41.9 %psum.28 = f32[64,64]{1,0:T(8,128)S(1)} all-reduce(f32[64,64]{1,0:T(8,128)S(1)} %convolution_bitcast_fusion.1), channel_id=1, replica_groups=mesh['gx'=16,'gy'=2] {'gx','gy'}, use_global_device_ids=true, to_apply=%region_0.0 | all-reduce | flops 4096 | bytes 32768 | tf_op jit(solution)/shard_map/psum | solution.py:82
  65.7 3.4 %fusion.1 = f32[64,4096]{1,0:T(8,128)} fusion(f32[64,4096]{0,1:T(8,128)S(1)} %bitcast.63, f32[64,4096]{1,0:T(8,128)S(1)} %copy.57, f32[]{:T(128)S(6)} %add.128, f32[64]{0:T(128)S(1)} %fusion.55, f32[64,64]{1,0:T(8,128)S(1)} %psum.28, f32[]{:T(128)S(6)} %mul.175, f32[64]{0:T(128)S(1)} %gather_fusion), kind=kOutput, calls=%fused_computation.6 | convolution fusion | flops 202133504 | bytes 3162632 | tf_op jit(solution)/shard_map/dot_general | solution.py:90
  70.5 2.4 %copy.35 = f32[64,2,2,512]{0,3,2,1:T(8,128)} copy(f32[64,2,2,512]{3,0,2,1:T(8,128)} %collective-permute-done.1) | data formatting | bytes 1048576 | tf_op jit(solution)/shard_map/ppermute | solution.py:25
  73.8 1.9 collective-permute-start.3
  77.0 2.4 %copy.38 = f32[4,4,64,1,128]{2,1,4,0,3:T(4,128)} copy(f32[4,4,64,1,128]{4,2,1,0,3:T(8,128)} %bitcast.78) | data formatting | bytes 1048576 | tf_op jit(solution)/shard_map/reshape | solution.py:53
  81.1 2.2 %fusion.8 = f32[64,2,6,514]{0,3,2,1:T(8,128)S(1)} fusion(f32[64,2,8,516]{0,3,2,1:T(8,128)S(1)} %pad_maximum_fusion, f32[64,2,8,2]{0,3,2,1:T(2,128)S(1)} %collective-permute-done.2, f32[64,2,2,512]{0,3,2,1:T(8,128)S(1)} %copy-done.1, f32[64,2,4,512]{0,3,2,1:T(8,128)S(1)} %broadcast_subtract_fusion.1, f32[64,2,2,512]{0,3,2,1:T(8,128)S(1)} %copy.34, ...), kind=kLoop, calls=%fused_computation.25 | loop fusion | flops 5131776 | bytes 8429568 | tf_op jit(solution)/shard_map/sub | solution.py:38
  84.6 2.4 %convolution_add_fusion.1 = f32[64,4096]{1,0:T(8,128)S(1)} fusion(f32[64,4096]{1,0:T(8,128)S(1)} %copy-done.3, f32[64,4096]{0,1:T(8,128)S(1)} %bitcast.67, f32[64,64]{1,0:T(8,128)S(1)} %psum.28, f32[]{:T(128)S(6)} %mul.175, f32[64]{0:T(128)S(1)} %gather_fusion), kind=kOutput, calls=%fused_computation.7 | convolution fusion | flops 201609216 | bytes 3162372 | tf_op jit(solution)/shard_map/dot_general | solution.py:89
  89.6 39.4 %all-reduce.2 = (f32[64,64]{1,0:T(8,128)S(1)}, f32[64,64]{0,1:T(8,128)S(1)}) all-reduce(f32[64,64]{1,0:T(8,128)S(1)} %fusion.29, f32[64,64]{0,1:T(8,128)S(1)} %fusion.27), channel_id=1, replica_groups=mesh['gx'=16,'gy'=2] {'gx','gy'}, use_global_device_ids=true, to_apply=%region_4.5 | all-reduce | flops 8192 | bytes 65536 | tf_op jit(solution)/shard_map/psum | solution.py:93
  130.4 1.9 copy.58
  132.3 3.5 %broadcast_subtract_fusion = (f32[64,2,4,512]{0,3,2,1:T(8,128)S(1)}, f32[64,2,4,512]{0,3,2,1:T(8,128)}) fusion(f32[2,4,512]{2,1,0:T(4,128)S(1)} %copy-done.7, f32[64,2,4,512]{0,3,2,1:T(8,128)} %copy.40, f32[64,2,4,512]{0,3,2,1:T(8,128)} %bitcast.70), kind=kLoop, calls=%fused_computation.63 | loop fusion | flops 524288 | bytes 4210688 | tf_op jit(solution)/shard_map/sub | solution.py:79
  136.9 2.4 %copy.44 = f32[64,2,2,512]{3,0,2,1:T(8,128)} copy(f32[64,2,2,512]{0,3,2,1:T(8,128)} %get-tuple-element.13) | data formatting | bytes 1048576 | tf_op jit(solution)/shard_map/slice | solution.py:23
  149.1 3.4 %fusion = f32[64,4096]{1,0:T(8,128)} fusion(f32[64,4096]{0,1:T(8,128)S(1)} %bitcast.66, f32[64,4096]{1,0:T(8,128)S(1)} %copy.59, f32[]{:T(128)S(6)} %add.146, f32[64]{0:T(128)S(1)} %fusion.56, f32[64,64]{1,0:T(8,128)S(1)} %fusion.48, f32[]{:T(128)S(6)} %mul.204, f32[64]{0:T(128)S(1)} %gather_fusion.1), kind=kOutput, calls=%fused_computation.3 | convolution fusion | flops 202133504 | bytes 3162632 | tf_op jit(solution)/shard_map/dot_general | solution.py:90
  155.2 2.4 %copy.47 = f32[64,2,2,512]{0,3,2,1:T(8,128)} copy(f32[64,2,2,512]{3,0,2,1:T(8,128)} %collective-permute-done.5) | data formatting | bytes 1048576 | tf_op jit(solution)/shard_map/ppermute | solution.py:25
  161.6 2.4 %copy.49 = f32[4,4,64,1,128]{2,1,4,0,3:T(4,128)} copy(f32[4,4,64,1,128]{4,2,1,0,3:T(8,128)} %bitcast.77) | data formatting | bytes 1048576 | tf_op jit(solution)/shard_map/reshape | solution.py:53
  165.8 2.2 %fusion.4 = f32[64,2,6,514]{0,3,2,1:T(8,128)S(1)} fusion(f32[64,2,8,516]{0,3,2,1:T(8,128)S(1)} %pad_maximum_fusion.1, f32[64,2,8,2]{0,3,2,1:T(2,128)S(1)} %collective-permute-done.6, f32[64,2,2,512]{0,3,2,1:T(8,128)S(1)} %copy-done, f32[64,2,4,512]{0,3,2,1:T(8,128)S(1)} %get-tuple-element.7, f32[64,2,2,512]{0,3,2,1:T(8,128)S(1)} %copy.46, ...), kind=kLoop, calls=%fused_computation.13 | loop fusion | flops 5131776 | bytes 8429568 | tf_op jit(solution)/shard_map/sub | solution.py:38
  169.3 3.1 %multiply_reduce_fusion = (f32[]{:T(128)}, f32[64,4096]{1,0:T(8,128)S(1)}) fusion(f32[64,4096]{1,0:T(8,128)S(1)} %copy-done.4, f32[64,4096]{0,1:T(8,128)S(1)} %bitcast.69, f32[64,64]{1,0:T(8,128)S(1)} %fusion.48, f32[]{:T(128)S(6)} %mul.204, f32[64]{0:T(128)S(1)} %gather_fusion.1), kind=kOutput, calls=%fused_computation.62 | convolution fusion | flops 202395648 | bytes 3162376 | tf_op jit(solution)/shard_map/dot_general | solution.py:89
  172.3 43.0 %psum.31 = f32[]{:T(128)} all-reduce(f32[]{:T(128)} %get-tuple-element.17), channel_id=1, replica_groups=mesh['gx'=16,'gy'=2] {'gx','gy'}, use_global_device_ids=true, to_apply=%region_11.12 | all-reduce | flops 1 | bytes 8 | tf_op jit(solution)/shard_map/psum | solution.py:59
  216.2 1.9 copy.60
  218.1 3.2 %add.157 = f32[64,2,4,512]{0,3,2,1:T(8,128)} add(f32[64,2,4,512]{0,3,2,1:T(8,128)S(1)} %copy-done.2, f32[64,2,4,512]{0,3,2,1:T(8,128)} %bitcast.68) | non-fusion elementwise | flops 262144 | bytes 3145728 | tf_op jit(solution)/shard_map/add | solution.py:104
  221.2 2.7 %copy.52 = f32[64,2,4,512]{3,2,1,0:T(4,128)} copy(f32[64,2,4,512]{0,3,2,1:T(8,128)} %add.157) | data formatting | bytes 2097152 | tf_op jit(solution)/shard_map/add | solution.py:104
  (80 shorter events, 41.9 us)
Async XLA Ops:
  0.0 2.8 %copy-start.7 = (f32[2,4,512]{2,1,0:T(4,128)S(1)}, f32[2,4,512]{2,1,0:T(4,128)}, u32[]{:S(2)}) copy-start(f32[2,4,512]{2,1,0:T(4,128)} %param.7) | copy-start | bytes 49156
  8.5 60.7 %collective-permute-start = (f32[64,2,2,512]{3,0,2,1:T(8,128)}, f32[64,2,2,512]{3,0,2,1:T(8,128)}, u32[]{:S(2)}, u32[]{:S(2)}) collective-permute-start(f32[64,2,2,512]{3,0,2,1:T(8,128)} %copy.32), channel_id=1, source_target_pairs={{0,2},{2,4},{4,6},{6,8},{8,10},{10,12},{12,14},{14,16},{16,18},{18... | collective-permute-start | bytes 1572872 | tf_op jit(solution)/shard_map/ppermute | solution.py:22
  9.6 60.9 %collective-permute-start.1 = (f32[64,2,2,512]{3,0,2,1:T(8,128)}, f32[64,2,2,512]{3,0,2,1:T(8,128)}, u32[]{:S(2)}, u32[]{:S(2)}) collective-permute-start(f32[64,2,2,512]{3,0,2,1:T(8,128)} %copy.33), channel_id=1, source_target_pairs={{2,0},{4,2},{6,4},{8,6},{10,8},{12,10},{14,12},{16,14},{18,16},{20... | collective-permute-start | bytes 1572872 | tf_op jit(solution)/shard_map/ppermute | solution.py:25
  13.2 3.6 %copy-start.8 = (s32[16,1,128]{2,1,0:T(1,128)S(1)}, s32[16,1,128]{2,1,0:T(1,128)}, u32[]{:S(2)}) copy-start(s32[16,1,128]{2,1,0:T(1,128)} %param.9) | copy-start | bytes 24580
  19.3 44.8 %copy-start.9 = (s32[1,128]{1,0:T(1,128)S(1)}, s32[1,128]{1,0:T(1,128)}, u32[]{:S(2)}) copy-start(s32[1,128]{1,0:T(1,128)} %param.8) | copy-start | bytes 1540
  61.2 4.5 %copy-start.10 = (f32[1,128]{1,0:T(1,128)S(1)}, f32[1,128]{1,0:T(1,128)}, u32[]{:S(2)}) copy-start(f32[1,128]{1,0:T(1,128)} %param.11) | copy-start | bytes 1540
  61.2 4.4 %copy-start.11 = (f32[1,128]{1,0:T(1,128)S(1)}, f32[1,128]{1,0:T(1,128)}, u32[]{:S(2)}) copy-start(f32[1,128]{1,0:T(1,128)} %param.10) | copy-start | bytes 1540
  73.7 5.7 %collective-permute-start.2 = (f32[64,2,8,2]{0,3,2,1:T(2,128)S(1)}, f32[64,2,8,2]{0,3,2,1:T(2,128)S(1)}, u32[]{:S(2)}, u32[]{:S(2)}) collective-permute-start(f32[64,2,8,2]{0,3,2,1:T(2,128)S(1)} %get-tuple-element.11), channel_id=1, source_target_pairs={{0,1},{1,0},{2,3},{3,2},{4,5},{5,4},{6,7},{7,6},{8,9},{9,8},{10,11... | collective-permute-start | bytes 24584 | tf_op jit(solution)/shard_map/ppermute | solution.py:22
  73.8 5.5 %collective-permute-start.3 = (f32[64,2,8,2]{0,3,2,1:T(2,128)S(1)}, f32[64,2,8,2]{0,3,2,1:T(2,128)S(1)}, u32[]{:S(2)}, u32[]{:S(2)}) collective-permute-start(f32[64,2,8,2]{0,3,2,1:T(2,128)S(1)} %get-tuple-element.12), channel_id=1, source_target_pairs={{1,0},{0,1},{3,2},{2,3},{5,4},{4,5},{7,6},{6,7},{9,8},{8,9},{11,10... | collective-permute-start | bytes 24584 | tf_op jit(solution)/shard_map/ppermute | solution.py:25
  79.3 1.8 copy-start.1
  81.1 2.3 %copy-start.6 = (f32[4,4,64,1,128]{2,1,4,0,3:T(4,128)S(1)}, f32[4,4,64,1,128]{2,1,4,0,3:T(4,128)}, u32[]{:S(2)}) copy-start(f32[4,4,64,1,128]{2,1,4,0,3:T(4,128)} %copy.38) | copy-start | bytes 1572868
  83.4 1.2 copy-start.3
  139.3 14.5 %collective-permute-start.4 = (f32[64,2,2,512]{3,0,2,1:T(8,128)}, f32[64,2,2,512]{3,0,2,1:T(8,128)}, u32[]{:S(2)}, u32[]{:S(2)}) collective-permute-start(f32[64,2,2,512]{3,0,2,1:T(8,128)} %copy.44), channel_id=1, source_target_pairs={{0,2},{2,4},{4,6},{6,8},{8,10},{10,12},{12,14},{14,16},{16,18},{18... | collective-permute-start | bytes 1572872 | tf_op jit(solution)/shard_map/ppermute | solution.py:22
  140.4 14.8 %collective-permute-start.5 = (f32[64,2,2,512]{3,0,2,1:T(8,128)}, f32[64,2,2,512]{3,0,2,1:T(8,128)}, u32[]{:S(2)}, u32[]{:S(2)}) collective-permute-start(f32[64,2,2,512]{3,0,2,1:T(8,128)} %copy.45), channel_id=1, source_target_pairs={{2,0},{4,2},{6,4},{8,6},{10,8},{12,10},{14,12},{16,14},{18,16},{20... | collective-permute-start | bytes 1572872 | tf_op jit(solution)/shard_map/ppermute | solution.py:25
  158.3 5.7 %collective-permute-start.6 = (f32[64,2,8,2]{0,3,2,1:T(2,128)S(1)}, f32[64,2,8,2]{0,3,2,1:T(2,128)S(1)}, u32[]{:S(2)}, u32[]{:S(2)}) collective-permute-start(f32[64,2,8,2]{0,3,2,1:T(2,128)S(1)} %get-tuple-element.9), channel_id=1, source_target_pairs={{0,1},{1,0},{2,3},{3,2},{4,5},{5,4},{6,7},{7,6},{8,9},{9,8},{10,11... | collective-permute-start | bytes 24584 | tf_op jit(solution)/shard_map/ppermute | solution.py:22
  159.6 4.4 %collective-permute-start.7 = (f32[64,2,8,2]{0,3,2,1:T(2,128)S(1)}, f32[64,2,8,2]{0,3,2,1:T(2,128)S(1)}, u32[]{:S(2)}, u32[]{:S(2)}) collective-permute-start(f32[64,2,8,2]{0,3,2,1:T(2,128)S(1)} %get-tuple-element.10), channel_id=1, source_target_pairs={{1,0},{0,1},{3,2},{2,3},{5,4},{4,5},{7,6},{6,7},{9,8},{8,9},{11,10... | collective-permute-start | bytes 24584 | tf_op jit(solution)/shard_map/ppermute | solution.py:25
  164.0 1.8 copy-start
  165.8 2.3 %copy-start.5 = (f32[4,4,64,1,128]{2,1,4,0,3:T(4,128)S(1)}, f32[4,4,64,1,128]{2,1,4,0,3:T(4,128)}, u32[]{:S(2)}) copy-start(f32[4,4,64,1,128]{2,1,4,0,3:T(4,128)} %copy.49) | copy-start | bytes 1572868
  168.0 1.2 copy-start.4
  216.1 1.9 copy-start.2
where the time goes:
time: 225 us; the launch traced here: 224 us
  blocking collectives  124 us (55%)
  local copies, waits for them, and re-layouts  40.5 us (18%)
  matrix products  23.9 us (11%)
  other arithmetic  23.2 us (10%)
  starting transfers between devices  7.67 us (3%)
  between operations  3.05 us (1%)
    psum x1, blocking collectives, norm_scale(): total = lax.psum(jnp.sum(drift * drift), ('gx', 'gy'))  43 us
    psum x1, blocking collectives, per_device(): lax.psum(jnp.dot(flat_dev, flat_dev.T, precision=highest), ('gx', 'gy'))  41.9 us
    psum x1, blocking collectives, per_device(): lax.psum((jnp.dot(flat_dev, drift.T, precision=highest), jnp.dot(drift, d...  39.4 us
    slice x4, local copies, waits for them, and re-layouts, with_halo(): lax.slice_in_dim(block, block.shape[dim] - width, None, axis=dim)  6.94 us
    dot_general x2, matrix products, per_device(): pulled = jnp.dot(kernel, flat_dev, precision=highest)  6.85 us
    ppermute x4, starting transfers between devices, with_halo(): lax.ppermute(lax.slice_in_dim(block, 0, width, axis=dim), axis, backward)  6.21 us
    sub x2, other arithmetic, per_device(): deviation = state - background[None]  5.68 us
    dot_general x2, matrix products, per_device(): attract = jnp.dot(kernel, flat_grad, precision=highest)  5.5 us
  transfers between devices with their start and end apart: 8, of which 1 were waited for; matrix products, arithmetic and copies ran while one was open for 17% of the time, Pallas kernels for 0%

commit v1 on v0

--- a/solution.py
+++ b/solution.py
@@ -79,7 +79,9 @@
         deviation = state - background[None]
         flat_dev = deviation.reshape(count, -1)
         if gram is None:
-            gram = lax.psum(jnp.dot(flat_dev, flat_dev.T, precision=highest), ("gx", "gy"))
+            block_2 = jnp.dot(flat_dev, flat_dev.T, precision=highest)
+            pieces = lax.all_gather(block_2, ("gx", "gy"), axis=0, tiled=False)
+            gram = pieces.sum(axis=0)
         gradient = prior_term(deviation) + observe_term(state, table, weights, values, variance)
         flat_grad = gradient.reshape(count, -1)
         diagonal = jnp.diagonal(gram)

time: 225 us -> 255 us (1.13)
  blocking collectives: 124 us -> 152 us
    all_gather x0 -> x1, blocking collectives: none -> 55 us  [per_device(): pieces = lax.all_gather(block_2, ('gx', 'gy'), axis=0, tiled=False)]
    psum x1 -> x0, blocking collectives: 41.9 us -> none  [per_device(): lax.psum(jnp.dot(flat_dev, flat_dev.T, precision=highest), ('gx', 'gy'))]
    psum x1, blocking collectives: 39.4 us -> 56.8 us  [per_device(): lax.psum((jnp.dot(flat_dev, drift.T, precision=highest), jnp.dot(drift, d...]
    psum x1, blocking collectives: 43 us -> 40.5 us  [norm_scale(): total = lax.psum(jnp.sum(drift * drift), ('gx', 'gy'))]
  transfers between devices with their start and end apart: 8 -> 8, of which waited for: 1 -> 1; matrix products, arithmetic and copies ran while one was open for 17% -> 15% of each run, Pallas kernels for 0% -> 0%
where the time goes in v1:
time: 255 us; the launch traced here: 252 us
  blocking collectives  152 us (60%)
  local copies, waits for them, and re-layouts  40.5 us (16%)
  matrix products  23.9 us (9%)
  other arithmetic  23.3 us (9%)
  starting transfers between devices  7.67 us (3%)
  between operations  3.05 us (1%)
    psum x1, blocking collectives, per_device(): lax.psum((jnp.dot(flat_dev, drift.T, precision=highest), jnp.dot(drift, d...  56.8 us
    all_gather x1, blocking collectives, per_device(): pieces = lax.all_gather(block_2, ('gx', 'gy'), axis=0, tiled=False)  55 us
    psum x1, blocking collectives, norm_scale(): total = lax.psum(jnp.sum(drift * drift), ('gx', 'gy'))  40.5 us
    slice x4, local copies, waits for them, and re-layouts, with_halo(): lax.slice_in_dim(block, block.shape[dim] - width, None, axis=dim)  6.92 us
    dot_general x2, matrix products, per_device(): pulled = jnp.dot(kernel, flat_dev, precision=highest)  6.85 us
    sub x2, other arithmetic, per_device(): deviation = state - background[None]  5.68 us
    ppermute x4, starting transfers between devices, with_halo(): lax.ppermute(lax.slice_in_dim(block, 0, width, axis=dim), axis, backward)  5.6 us
    dot_general x2, matrix products, per_device(): attract = jnp.dot(kernel, flat_grad, precision=highest)  5.5 us
  transfers between devices with their start and end apart: 8, of which 1 were waited for; matrix products, arithmetic and copies ran while one was open for 15% of the time, Pallas kernels for 0%

profile of v1, /device:TPU:14, one launch (start us, length us, event | category | flops | bytes accessed | tf_op | source)
XLA Modules:
  0.0 252.0 jit_solution(482518923436061661)
XLA Ops:
  0.0 2.8 %copy.40 = f32[64,2,4,512]{0,3,2,1:T(8,128)} copy(f32[64,2,4,512]{3,2,1,0:T(4,128)} %param.6) | data formatting | bytes 2097152 | tf_op args[0]
  2.8 2.2 broadcast_subtract_fusion.1
  6.1 2.4 copy.32
  11.3 1.9 slice.112
  13.2 3.6 %convolution_bitcast_fusion.1 = f32[64,64]{1,0:T(8,128)S(1)} fusion(f32[64,2,4,512]{0,3,2,1:T(8,128)S(1)} %broadcast_subtract_fusion.1), kind=kOutput, calls=%fused_computation.61 | convolution fusion | flops 201326592 | bytes 1064960 | tf_op jit(solution)/shard_map/dot_general | solution.py:82
  19.3 55.0 %all-gather = f32[2048,64]{1,0:T(8,128)S(1)} all-gather(f32[64,64]{1,0:T(8,128)S(1)} %convolution_bitcast_fusion.1), channel_id=2, replica_groups=mesh['gx'=16,'gy'=2] {'gx','gy'}, dimensions={0}, use_global_device_ids=true | all-gather | bytes 540672 | tf_op jit(solution)/shard_map/all_gather | solution.py:83
  79.0 3.4 %fusion.1 = f32[64,4096]{1,0:T(8,128)} fusion(f32[64,4096]{0,1:T(8,128)S(1)} %bitcast.64, f32[64,4096]{1,0:T(8,128)S(1)} %copy.57, f32[]{:T(128)S(6)} %add.126, f32[64]{0:T(128)S(1)} %fusion.55, f32[64,64]{1,0:T(8,128)S(1)} %reduce_sum.82, f32[]{:T(128)S(6)} %mul.175, f32[64]{0:T(128)S(1)} %gather_fusion), kind=kOutput, calls=%fused_computation.6 | convolution fusion | flops 202133504 | bytes 3162632 | tf_op jit(solution)/shard_map/dot_general | solution.py:92
  83.8 2.4 copy.35
  90.2 2.4 copy.38
  94.4 2.2 fusion.8
  97.9 2.4 convolution_add_fusion.1
  102.8 56.8 %all-reduce.2 = (f32[64,64]{1,0:T(8,128)S(1)}, f32[64,64]{0,1:T(8,128)S(1)}) all-reduce(f32[64,64]{1,0:T(8,128)S(1)} %fusion.29, f32[64,64]{0,1:T(8,128)S(1)} %fusion.27), channel_id=1, replica_groups=mesh['gx'=16,'gy'=2] {'gx','gy'}, use_global_device_ids=true, to_apply=%region_4.5 | all-reduce | flops 8192 | bytes 65536 | tf_op jit(solution)/shard_map/psum | solution.py:95
  161.0 1.9 copy.58
  162.9 3.5 %broadcast_subtract_fusion = (f32[64,2,4,512]{0,3,2,1:T(8,128)S(1)}, f32[64,2,4,512]{0,3,2,1:T(8,128)}) fusion(f32[2,4,512]{2,1,0:T(4,128)S(1)} %copy-done.7, f32[64,2,4,512]{0,3,2,1:T(8,128)} %copy.40, f32[64,2,4,512]{0,3,2,1:T(8,128)} %bitcast.71), kind=kLoop, calls=%fused_computation.63 | loop fusion | flops 524288 | bytes 4210688 | tf_op jit(solution)/shard_map/sub | solution.py:79
  167.5 2.4 copy.44
  179.7 3.4 %fusion = f32[64,4096]{1,0:T(8,128)} fusion(f32[64,4096]{0,1:T(8,128)S(1)} %bitcast.67, f32[64,4096]{1,0:T(8,128)S(1)} %copy.59, f32[]{:T(128)S(6)} %add.144, f32[64]{0:T(128)S(1)} %fusion.56, f32[64,64]{1,0:T(8,128)S(1)} %fusion.48, f32[]{:T(128)S(6)} %mul.204, f32[64]{0:T(128)S(1)} %gather_fusion.1), kind=kOutput, calls=%fused_computation.3 | convolution fusion | flops 202133504 | bytes 3162632 | tf_op jit(solution)/shard_map/dot_general | solution.py:92
  185.8 2.4 copy.47
  192.2 2.4 copy.49
  196.4 2.2 fusion.4
  199.9 3.1 %multiply_reduce_fusion = (f32[]{:T(128)}, f32[64,4096]{1,0:T(8,128)S(1)}) fusion(f32[64,4096]{1,0:T(8,128)S(1)} %copy-done.4, f32[64,4096]{0,1:T(8,128)S(1)} %bitcast.70, f32[64,64]{1,0:T(8,128)S(1)} %fusion.48, f32[]{:T(128)S(6)} %mul.204, f32[64]{0:T(128)S(1)} %gather_fusion.1), kind=kOutput, calls=%fused_computation.62 | convolution fusion | flops 202395648 | bytes 3162376 | tf_op jit(solution)/shard_map/dot_general | solution.py:91
  202.9 40.5 %psum.23 = f32[]{:T(128)} all-reduce(f32[]{:T(128)} %get-tuple-element.17), channel_id=1, replica_groups=mesh['gx'=16,'gy'=2] {'gx','gy'}, use_global_device_ids=true, to_apply=%region_11.12 | all-reduce | flops 1 | bytes 8 | tf_op jit(solution)/shard_map/psum | solution.py:59
  244.2 1.9 copy.60
  246.1 3.2 %add.155 = f32[64,2,4,512]{0,3,2,1:T(8,128)} add(f32[64,2,4,512]{0,3,2,1:T(8,128)S(1)} %copy-done.2, f32[64,2,4,512]{0,3,2,1:T(8,128)} %bitcast.69) | non-fusion elementwise | flops 262144 | bytes 3145728 | tf_op jit(solution)/shard_map/add | solution.py:106
  249.3 2.7 %copy.52 = f32[64,2,4,512]{3,2,1,0:T(4,128)} copy(f32[64,2,4,512]{0,3,2,1:T(8,128)} %add.155) | data formatting | bytes 2097152 | tf_op jit(solution)/shard_map/add | solution.py:106
  (81 shorter events, 42.0 us)
Async XLA Ops:
  0.0 2.8 %copy-start.7 = (f32[2,4,512]{2,1,0:T(4,128)S(1)}, f32[2,4,512]{2,1,0:T(4,128)}, u32[]{:S(2)}) copy-start(f32[2,4,512]{2,1,0:T(4,128)} %param.7) | copy-start | bytes 49156
  8.5 73.9 %collective-permute-start = (f32[64,2,2,512]{3,0,2,1:T(8,128)}, f32[64,2,2,512]{3,0,2,1:T(8,128)}, u32[]{:S(2)}, u32[]{:S(2)}) collective-permute-start(f32[64,2,2,512]{3,0,2,1:T(8,128)} %copy.32), channel_id=1, source_target_pairs={{0,2},{2,4},{4,6},{6,8},{8,10},{10,12},{12,14},{14,16},{16,18},{18... | collective-permute-start | bytes 1572872 | tf_op jit(solution)/shard_map/ppermute | solution.py:22
  9.6 74.2 %collective-permute-start.1 = (f32[64,2,2,512]{3,0,2,1:T(8,128)}, f32[64,2,2,512]{3,0,2,1:T(8,128)}, u32[]{:S(2)}, u32[]{:S(2)}) collective-permute-start(f32[64,2,2,512]{3,0,2,1:T(8,128)} %copy.33), channel_id=1, source_target_pairs={{2,0},{4,2},{6,4},{8,6},{10,8},{12,10},{14,12},{16,14},{18,16},{20... | collective-permute-start | bytes 1572872 | tf_op jit(solution)/shard_map/ppermute | solution.py:25
  13.2 3.6 %copy-start.8 = (s32[16,1,128]{2,1,0:T(1,128)S(1)}, s32[16,1,128]{2,1,0:T(1,128)}, u32[]{:S(2)}) copy-start(s32[16,1,128]{2,1,0:T(1,128)} %param.9) | copy-start | bytes 24580
  74.5 2.9 %copy-start.9 = (s32[1,128]{1,0:T(1,128)S(1)}, s32[1,128]{1,0:T(1,128)}, u32[]{:S(2)}) copy-start(s32[1,128]{1,0:T(1,128)} %param.8) | copy-start | bytes 1540
  74.5 4.5 %copy-start.10 = (f32[1,128]{1,0:T(1,128)S(1)}, f32[1,128]{1,0:T(1,128)}, u32[]{:S(2)}) copy-start(f32[1,128]{1,0:T(1,128)} %param.11) | copy-start | bytes 1540
  74.5 4.5 %copy-start.11 = (f32[1,128]{1,0:T(1,128)S(1)}, f32[1,128]{1,0:T(1,128)}, u32[]{:S(2)}) copy-start(f32[1,128]{1,0:T(1,128)} %param.10) | copy-start | bytes 1540
  86.9 5.7 %collective-permute-start.2 = (f32[64,2,8,2]{0,3,2,1:T(2,128)S(1)}, f32[64,2,8,2]{0,3,2,1:T(2,128)S(1)}, u32[]{:S(2)}, u32[]{:S(2)}) collective-permute-start(f32[64,2,8,2]{0,3,2,1:T(2,128)S(1)} %get-tuple-element.11), channel_id=1, source_target_pairs={{0,1},{1,0},{2,3},{3,2},{4,5},{5,4},{6,7},{7,6},{8,9},{9,8},{10,11... | collective-permute-start | bytes 24584 | tf_op jit(solution)/shard_map/ppermute | solution.py:22
  87.3 5.3 %collective-permute-start.3 = (f32[64,2,8,2]{0,3,2,1:T(2,128)S(1)}, f32[64,2,8,2]{0,3,2,1:T(2,128)S(1)}, u32[]{:S(2)}, u32[]{:S(2)}) collective-permute-start(f32[64,2,8,2]{0,3,2,1:T(2,128)S(1)} %get-tuple-element.12), channel_id=1, source_target_pairs={{1,0},{0,1},{3,2},{2,3},{5,4},{4,5},{7,6},{6,7},{9,8},{8,9},{11,10... | collective-permute-start | bytes 24584 | tf_op jit(solution)/shard_map/ppermute | solution.py:25
  92.6 1.8 copy-start.1
  94.4 2.3 copy-start.6
  96.6 1.2 copy-start.3
  169.9 14.5 %collective-permute-start.4 = (f32[64,2,2,512]{3,0,2,1:T(8,128)}, f32[64,2,2,512]{3,0,2,1:T(8,128)}, u32[]{:S(2)}, u32[]{:S(2)}) collective-permute-start(f32[64,2,2,512]{3,0,2,1:T(8,128)} %copy.44), channel_id=1, source_target_pairs={{0,2},{2,4},{4,6},{6,8},{8,10},{10,12},{12,14},{14,16},{16,18},{18... | collective-permute-start | bytes 1572872 | tf_op jit(solution)/shard_map/ppermute | solution.py:22
  171.0 14.8 %collective-permute-start.5 = (f32[64,2,2,512]{3,0,2,1:T(8,128)}, f32[64,2,2,512]{3,0,2,1:T(8,128)}, u32[]{:S(2)}, u32[]{:S(2)}) collective-permute-start(f32[64,2,2,512]{3,0,2,1:T(8,128)} %copy.45), channel_id=1, source_target_pairs={{2,0},{4,2},{6,4},{8,6},{10,8},{12,10},{14,12},{16,14},{18,16},{20... | collective-permute-start | bytes 1572872 | tf_op jit(solution)/shard_map/ppermute | solution.py:25
  188.9 5.7 %collective-permute-start.6 = (f32[64,2,8,2]{0,3,2,1:T(2,128)S(1)}, f32[64,2,8,2]{0,3,2,1:T(2,128)S(1)}, u32[]{:S(2)}, u32[]{:S(2)}) collective-permute-start(f32[64,2,8,2]{0,3,2,1:T(2,128)S(1)} %get-tuple-element.9), channel_id=1, source_target_pairs={{0,1},{1,0},{2,3},{3,2},{4,5},{5,4},{6,7},{7,6},{8,9},{9,8},{10,11... | collective-permute-start | bytes 24584 | tf_op jit(solution)/shard_map/ppermute | solution.py:22
  190.5 4.1 %collective-permute-start.7 = (f32[64,2,8,2]{0,3,2,1:T(2,128)S(1)}, f32[64,2,8,2]{0,3,2,1:T(2,128)S(1)}, u32[]{:S(2)}, u32[]{:S(2)}) collective-permute-start(f32[64,2,8,2]{0,3,2,1:T(2,128)S(1)} %get-tuple-element.10), channel_id=1, source_target_pairs={{1,0},{0,1},{3,2},{2,3},{5,4},{4,5},{7,6},{6,7},{9,8},{8,9},{11,10... | collective-permute-start | bytes 24584 | tf_op jit(solution)/shard_map/ppermute | solution.py:25
  194.6 1.8 copy-start
  196.4 2.3 copy-start.5
  198.7 1.2 copy-start.4
  244.2 1.9 copy-start.2
